TPU v7x, 128 devices: a whole 4x4x4 slice. The times are simulated.
128 devices in a mesh: pb: 8 (over z, core), pa: 16 (over y, x).
Axes of the slice: x: 4, y: 4, z: 4, core: 2. Of those that a mesh axis runs over, the one named last changes fastest.
Arguments:
- queries: bfloat16 [16384, 3584], P(('pb', 'pa')), may hold values from -16 to 16
- passages: bfloat16 [65536, 3584], P(('pb', 'pa')), may hold values from -16 to 16
- hard_block_offsets: int32 [4096, 4], P(('pb', 'pa')), may hold values from 0 to 126, all different within a row; in each aligned block of 32 rows (0 to 31, 32 to 63, ...) at most 2 rows name the same one
- positive: int32 [16384], P(('pb', 'pa')), may hold values from 0 to 511
- context: bfloat16 [65536, 3584], P(('pb', 'pa')), may hold values from -24 to 24
- residual: bfloat16 [65536, 3584], P(('pb', 'pa')), may hold values from -6 to 6
- output_weight: bfloat16 [3584, 3584], P(('pb', 'pa')), may hold values from -0.09375 to 0.09375
- adapter_down_weight: bfloat16 [3584, 16], replicated, may hold values from -0.09375 to 0.09375
- adapter_up_weight: bfloat16 [16, 3584], replicated, may hold values from -1.5 to 1.5
- final_norm_weight: bfloat16 [3584], replicated, may hold values from 0.099609375 to 1.8984375
Outputs:
- query_gradient: float32 [16384, 3584], P(('pb', 'pa'))
- grad_passages: float32 [65536, 3584], P(('pb', 'pa'))
- grad_lora_down: float32 [3584, 16], P(('pb', 'pa'))
- grad_lora_up: float32 [16, 3584], P(None, ('pb', 'pa'))
Inputs may be any that keep to these rules, and one draw needn't show every extreme that they name: `hard_block_offsets`: each row lists 4 different offsets. Query block k is paired with passage block (k // 32 + 1 + offset) modulo the number of devices. In each aligned block of 32 rows no offset appears more than 2 times, and some offset appears exactly 2 times.
All inputs are finite; a program needn't handle non-finite values.
Results may differ from a plain program's by a relative error of at most 0.0045.
Values may be sent and summed in bfloat16 or wider, within the bound.
A program may use at most 192 MiB of HBM per device.

v0:
```python
import math
import jax
import jax.numpy as jnp
from jax import lax
from jax.sharding import Mesh
from jax.sharding import PartitionSpec as P

MODEL_WIDTH = 3584
RERUN_QUERIES = 16
TQ = 32
PB_PA = ("pb_0", "pb_1", "pa_0", "pa_1")
CHIPS = ("pb_0", "pa_0", "pa_1")
inverse_temp = 2.0
loss_scale = 32.0
adapter_scale = 2.0
epsilon = 1e-06
absent_mass = 1e30
f32 = jnp.float32
bf16 = jnp.bfloat16


def dot(a, b, **kw):
    return jnp.dot(a, b, preferred_element_type=f32, **kw)


def two_parts(x):
    high = x.astype(bf16)
    return (high, (x - high.astype(f32)).astype(bf16))


def device_of(chip, core, per_plane):
    return chip // per_plane * 2 * per_plane + core * per_plane + chip % per_plane


def gathered_weight_input(rows):
    count = lax.axis_size(PB_PA)
    per_plane = lax.axis_size("pa_0") * lax.axis_size("pa_1")
    half = rows.shape[1] // 2
    left, right = (rows[:, :half], rows[:, half:])
    odd = lax.axis_index("pa_1") % 2 == 1
    core = lax.axis_index("pb_1")
    same = [(f, device_of(f // 2, f % 2, per_plane)) for f in range(count)]
    other = [(f, device_of(f // 2, 1 - f % 2, per_plane)) for f in range(count)]
    first = lax.ppermute(jnp.where(odd, right, left), PB_PA, same)
    second = lax.ppermute(jnp.where(odd, left, right), PB_PA, other)
    low = jnp.where(core == 0, first, second)
    high = jnp.where(core == 0, second, first)
    return jnp.concatenate([low, high], axis=0)


def exchange(array):
    return lax.all_to_all(array, PB_PA, split_axis=0, concat_axis=0, tiled=True)


def local(
    queries,
    passages,
    hard_block_offsets,
    positive,
    context,
    residual,
    output_weight,
    adapter_down_weight,
    adapter_up_weight,
    final_norm_weight,
):
    device_count = lax.axis_size(PB_PA)
    block_count, hard_count = hard_block_offsets.shape
    query_count = queries.shape[0]
    block_rows = query_count // block_count
    capacity = 2 * block_count * hard_count // device_count
    slot_rows = capacity * block_rows
    all_rows = device_count * slot_rows
    passage_count = passages.shape[0]
    score_scale = inverse_temp / math.sqrt(MODEL_WIDTH)
    weight_rows = gathered_weight_input(output_weight)
    source = lax.axis_index(PB_PA)
    target = ((source + 1 + hard_block_offsets) % device_count).reshape(-1)
    order = jnp.arange(target.shape[0], dtype=jnp.int32)
    earlier = (target[:, None] == target[None, :]) & (order[:, None] > order[None, :])
    slot = target * capacity + jnp.sum(earlier.astype(jnp.int32), axis=1)
    slot_of = slot.reshape(block_count, hard_count).T
    key = (
        jnp.repeat(slot_of, block_rows, axis=1) * block_rows
        + jnp.arange(query_count, dtype=jnp.int32) % block_rows
    )
    row_ids = jnp.arange(all_rows, dtype=jnp.int32)
    picks = row_ids[:, None] == key[0][None, :]
    for t in range(1, hard_count):
        picks = picks | (row_ids[:, None] == key[t][None, :])
    outgoing = jnp.dot(picks.astype(bf16), queries, preferred_element_type=bf16)
    arrived = exchange(outgoing.reshape(device_count, slot_rows, MODEL_WIDTH))
    arrived = arrived.reshape(-1, MODEL_WIDTH)
    half_weight = lax.all_gather(weight_rows, CHIPS, axis=0, tiled=True)
    near_scores = dot(queries, passages.T) * score_scale
    near_peak = jnp.max(near_scores, axis=1)
    near_exp = jnp.exp(near_scores - near_peak[:, None])
    near_sum = jnp.sum(near_exp, axis=1)
    near_mass = near_peak + jnp.log(near_sum)
    positive_hot = positive[:, None] == jnp.arange(passage_count, dtype=jnp.int32)[None, :]
    stacked = dot(
        jnp.concatenate([near_exp.astype(bf16), positive_hot.astype(bf16)], axis=0), passages
    )
    far_scores = dot(arrived, passages.T) * score_scale
    far_peak = jnp.max(far_scores, axis=1)
    far_exp = jnp.exp(far_scores - far_peak[:, None])
    far_sum = jnp.sum(far_exp, axis=1)
    far_mass = far_peak + jnp.log(far_sum)
    far_mean = (dot(far_exp.astype(bf16), passages) / far_sum[:, None]).astype(bf16)
    returned = exchange(far_mean.reshape(device_count, slot_rows, MODEL_WIDTH))
    returned = returned.reshape(-1, MODEL_WIDTH)
    far_mass, _ = lax.optimization_barrier((far_mass, far_mean))
    returned_mass = exchange(far_mass.reshape(device_count, slot_rows)).reshape(-1)
    half_weight, returned_mass = lax.optimization_barrier((half_weight, returned_mass))
    both_halves = lax.all_gather(half_weight, "pb_1", axis=0, tiled=False)
    hits = [key[t][:, None] == row_ids[None, :] for t in range(hard_count)]
    masses = [near_mass] + [
        jnp.sum(jnp.where(hit, returned_mass[None, :], 0.0), axis=1) for hit in hits
    ]
    peak = masses[0]
    for mass in masses[1:]:
        peak = jnp.maximum(peak, mass)
    total = jnp.exp(masses[0] - peak)
    for mass in masses[1:]:
        total = total + jnp.exp(mass - peak)
    log_total = peak + jnp.log(total)
    filled = jnp.any(picks, axis=1)
    log_outgoing = jnp.where(
        filled, jnp.sum(jnp.where(picks, log_total[None, :], 0.0), axis=1), absent_mass
    )
    log_arrived = exchange(log_outgoing.reshape(device_count, slot_rows)).reshape(-1)
    mix = jnp.zeros((query_count, all_rows), f32)
    for t in range(hard_count):
        mix = jnp.where(hits[t], jnp.exp(masses[1 + t] - log_total)[:, None], mix)
    mix_parts = jnp.concatenate(two_parts(mix), axis=0)
    near_share = jnp.exp(near_mass - log_total)
    near_part = (near_share / near_sum)[:, None] * stacked[:query_count] - stacked[query_count:]
    product_dims = (((0,), (0,)), ((), ()))
    far_weight = jnp.exp(far_scores - log_arrived[:, None]).astype(bf16)
    near_weight = (jnp.exp(near_scores - log_total[:, None]) - positive_hot.astype(f32)).astype(
        bf16
    )
    far_grad = lax.dot_general(far_weight, arrived, product_dims, preferred_element_type=f32)
    near_grad = lax.dot_general(near_weight, queries, product_dims, preferred_element_type=f32)
    grad_passages = loss_scale * score_scale * (far_grad + near_grad)
    narrow = dot(context, adapter_down_weight).astype(bf16)
    frozen = jnp.concatenate([dot(context, both_halves[0]), dot(context, both_halves[1])], axis=1)
    hidden = residual.astype(f32) + frozen + adapter_scale * dot(narrow, adapter_up_weight)
    inverse_rms = lax.rsqrt(jnp.mean(hidden * hidden, axis=1, keepdims=True) + epsilon)
    hidden_low = hidden.astype(bf16)
    hidden_up = dot(hidden_low, adapter_up_weight.T)
    token_query = jnp.arange(context.shape[0], dtype=jnp.int32) // TQ
    of_query = token_query[:, None] == jnp.arange(RERUN_QUERIES, dtype=jnp.int32)[None, :]
    narrow_sums = jnp.sum((inverse_rms * narrow.astype(f32)).reshape(RERUN_QUERIES, TQ, -1), axis=1)
    returned, hidden_low, hidden_up, inverse_rms, narrow_sums = lax.optimization_barrier(
        (returned, hidden_low, hidden_up, inverse_rms, narrow_sums)
    )
    far_part = dot(mix_parts, returned)
    query_gradient = (
        loss_scale * score_scale * (far_part[:query_count] + far_part[query_count:] + near_part)
    )
    scaled = final_norm_weight.astype(f32)[None, :] * (query_gradient[:RERUN_QUERIES] / TQ)
    products = dot(hidden_low, scaled.astype(bf16).T)
    mean = jnp.sum(jnp.where(of_query, products, 0.0), axis=1, keepdims=True) / MODEL_WIDTH
    slope = inverse_rms**3 * mean
    scaled_up = dot(scaled, adapter_up_weight.astype(f32).T, precision=lax.Precision.HIGHEST)
    spread_up = jnp.broadcast_to(
        scaled_up[:, None, :], (RERUN_QUERIES, TQ, scaled_up.shape[1])
    ).reshape(context.shape[0], -1)
    grad_narrow = (adapter_scale * (inverse_rms * spread_up - slope * hidden_up)).astype(bf16)
    down_term = lax.dot_general(grad_narrow, context, product_dims, preferred_element_type=f32)
    weighted = (slope * narrow.astype(f32)).astype(bf16)
    up_term = adapter_scale * (
        lax.dot_general(
            narrow_sums,
            scaled,
            product_dims,
            precision=lax.Precision.HIGHEST,
            preferred_element_type=f32,
        )
        - lax.dot_general(weighted, hidden_low, product_dims, preferred_element_type=f32)
    )
    terms = jnp.concatenate([down_term, up_term], axis=0) / RERUN_QUERIES
    rank = narrow.shape[1]
    columns = MODEL_WIDTH // device_count
    pieces = jnp.transpose(terms.reshape(2 * rank, device_count, columns), (1, 0, 2))
    sums = jnp.sum(exchange(pieces.reshape(device_count, -1)), axis=0).reshape(2 * rank, columns)
    return (query_gradient, grad_passages, sums[:rank].T, sums[rank:])


def solution(mesh):
    torus = Mesh(mesh.devices.reshape(4, 2, 4, 4), PB_PA)
    in_specs = (
        P(PB_PA, None),
        P(PB_PA, None),
        P(PB_PA, None),
        P(PB_PA),
        P(PB_PA, None),
        P(PB_PA, None),
        P(PB_PA, None),
        P(),
        P(),
        P(),
    )
    out_specs = (P(PB_PA, None), P(PB_PA, None), P(PB_PA, None), P(None, PB_PA))
    return jax.shard_map(local, mesh=torus, in_specs=in_specs, out_specs=out_specs, check_vma=False)
```

profile of v0, /device:TPU:1, one launch (start us, length us, event | category | flops | bytes accessed | tf_op | source)
XLA Modules:
  0.0 347.3 jit_solution(11407724801208197337)
XLA Ops:
  7.2 1.0 broadcast_select_fusion.1
  8.3 6.2 %collective-permute-start = (bf16[28,1792]{1,0:T(8,128)(2,1)S(1)}, bf16[28,1792]{1,0:T(8,128)(2,1)S(1)}, u32[]{:S(2)}, u32[]{:S(2)}) collective-permute-start(bf16[28,1792]{1,0:T(8,128)(2,1)S(1)} %get-tuple-element.32), channel_id=1, source_target_pairs={{0,0},{1,16},{2,1},{3,17},{4,2},{5,18},{6,3},{7,19},{8,4},{9,20},{... | collective-permute-start | bytes 301064 | tf_op jit(solution)/shard_map/ppermute | solution.py:44
  14.5 1.1 collective-permute-start.1
  15.6 3.1 collective-permute-done
  18.7 1.2 collective-permute-done.1
  19.9 0.7 pad_maximum_fusion
  20.7 0.8 copy.36
  22.3 2.1 convolution_bitcast_fusion
  24.3 109.4 %all_to_all.34 = bf16[128,8,3584]{2,1,0:T(8,128)(2,1)S(1)} all-to-all(bf16[128,8,3584]{2,1,0:T(8,128)(2,1)S(1)} %convolution_bitcast_fusion), channel_id=1, replica_groups=mesh['pb_0'=4,'pb_1'=2,'pa_0'=4,'pa_1'=4] {'pb_0','pb_1','pa_0','pa_1'}, dimensions={0} | all-to-all | bytes 14680064 | tf_op jit(solution)/shard_map/all_to_all | solution.py:52
  133.8 4.0 %multiply_reduce_fusion.1 = (f32[1024]{0:T(1024)S(1)}, f32[1024,512]{0,1:T(8,128)S(1)}) fusion(bf16[512,3584]{1,0:T(8,128)(2,1)S(1)} %copy-done.2, bf16[128,8,3584]{2,1,0:T(8,128)(2,1)S(1)} %all_to_all.34), kind=kOutput, calls=%fused_computation.27 | convolution fusion | flops 3759143936 | bytes 13111296 | tf_op jit(solution)/shard_map/dot_general | solution.py:23
  137.8 0.4 fusion.17
  138.2 1.0 copy-done.9
  139.1 6.1 %divide_convert_fusion = bf16[1024,3584]{1,0:T(8,128)(2,1)} fusion(f32[1024]{0:T(1024)S(1)} %fusion.17, bf16[512,3584]{1,0:T(8,128)(2,1)S(1)} %copy-done.2, f32[1024,512]{0,1:T(8,128)S(1)} %get-tuple-element.47, f32[1024]{0:T(1024)S(1)} %get-tuple-element.46), kind=kOutput, calls=%fused_computation | convolution fusion | flops 3767009280 | bytes 13115392 | tf_op jit(solution)/shard_map/dot_general | solution.py:23
  145.3 17.4 %all_to_all.35 = f32[128,1,8]{2,1,0:T(1,128)S(1)} all-to-all(f32[128,1,8]{2,1,0:T(1,128)S(1)} %bitcast.62), channel_id=1, replica_groups=mesh['pb_0'=4,'pb_1'=2,'pa_0'=4,'pa_1'=4] {'pb_0','pb_1','pa_0','pa_1'}, dimensions={0} | all-to-all | bytes 8192 | tf_op jit(solution)/shard_map/all_to_all | solution.py:52
  162.7 0.5 broadcast.136
  163.2 0.8 reduce.7
  164.1 16.1 %all-gather.4.cloned.1.call-done = bf16[3584,1792]{1,0:T(8,128)(2,1)} async-done(((bf16[56,1792]{1,0:T(8,128)(2,1)}), bf16[3584,1792]{1,0:T(8,128)(2,1)}) %all-gather.4.cloned.1.call-update) | async-done | bytes 12845072 | tf_op jit(solution)/shard_map/all_gather | solution.py:94
  180.6 3.4 fusion.72
  184.2 0.4 select_reduce_fusion.2
  185.0 17.2 %all_to_all.36 = f32[128,1,8]{2,1,0:T(1,128)S(1)} all-to-all(f32[128,1,8]{2,1,0:T(1,128)S(1)} %bitcast.63), channel_id=1, replica_groups=mesh['pb_0'=4,'pb_1'=2,'pa_0'=4,'pa_1'=4] {'pb_0','pb_1','pa_0','pa_1'}, dimensions={0} | all-to-all | bytes 8192 | tf_op jit(solution)/shard_map/all_to_all | solution.py:52
  202.3 5.9 %all-to-all-start.2 = ((bf16[128,8,3584]{2,1,0:T(8,128)(2,1)}), bf16[128,8,3584]{2,1,0:T(8,128)(2,1)}, u32[]{:S(2)}, u32[]{:S(2)}) async-start(bf16[128,8,3584]{2,1,0:T(8,128)(2,1)} %bitcast.61), calls=%async_computation.2 | async-start | bytes 14680064 | tf_op jit(solution)/shard_map/all_to_all | solution.py:52
  208.2 6.3 %copy.39 = bf16[512,3584]{0,1:T(8,128)(2,1)} copy(bf16[512,3584]{1,0:T(8,128)(2,1)} %param.15) | data formatting | bytes 7340032 | tf_op args[5]
  214.6 3.2 convolution_convert_fusion
  217.8 3.1 fusion.35
  221.6 0.8 reduce.8
  222.5 10.6 %fusion.5 = f32[512,3584]{1,0:T(8,128)} fusion(bf16[128,8,3584]{2,1,0:T(8,128)(2,1)} %copy-done.6, f32[1024,512]{0,1:T(8,128)} %copy-done.9, f32[1024]{0:T(1024)S(1)} %sub.236), kind=kOutput, calls=%fused_computation.7 | convolution fusion | flops 3759669248 | bytes 16781312 | tf_op jit(solution)/shard_map/dot_general | solution.py:143
  233.1 12.7 %fusion.10 = f32[512,1792]{0,1:T(8,128)S(1)} fusion(bf16[512,3584]{1,0:T(8,128)(2,1)} %param.14, bf16[7168,1792]{1,0:T(8,128)(2,1)} %all-gather.6.cloned.1.call-done), kind=kOutput, calls=%fused_computation.16 | convolution fusion | flops 6576668672 | bytes 20185088 | tf_op jit(solution)/shard_map/dot_general | solution.py:23
  245.8 10.3 %fusion.13 = f32[512,1792]{0,1:T(8,128)S(1)} fusion(bf16[512,3584]{1,0:T(8,128)(2,1)S(1)} %copy-done.4, bf16[7168,1792]{1,0:T(8,128)(2,1)} %all-gather.6.cloned.1.call-done), kind=kOutput, calls=%fused_computation.17 | convolution fusion | flops 6576668672 | bytes 20185088 | tf_op jit(solution)/shard_map/dot_general | solution.py:23
  256.2 3.6 %multiply_reduce_fusion = (f32[512]{0:T(512)S(1)}, bf16[512,3584]{0,1:T(8,128)(2,1)}) fusion(bf16[512,16]{0,1:T(8,128)(2,1)S(1)} %convolution_convert_fusion, bf16[16,3584]{1,0:T(8,128)(2,1)S(1)} %copy-done.10, f32[512,1792]{0,1:T(8,128)S(1)} %fusion.13, f32[512,1792]{0,1:T(8,128)S(1)} %fusion.10, bf16[512,3584]{0,1:T(8,128)(2,1)S(1)} %copy-done.7), kind=kOutput, calls=%fused_computation.12 | convolution fusion | flops 73399808 | bytes 14813184 | tf_op jit(solution)/shard_map/dot_general | solution.py:23
  260.0 2.6 fusion.73
  262.6 32.0 %all-to-all-done.2 = bf16[128,8,3584]{2,1,0:T(8,128)(2,1)} async-done(((bf16[128,8,3584]{2,1,0:T(8,128)(2,1)}), bf16[128,8,3584]{2,1,0:T(8,128)(2,1)}, u32[]{:S(2)}, u32[]{:S(2)}) %all-to-all-start.2) | async-done | bytes 7340064 | tf_op jit(solution)/shard_map/all_to_all | solution.py:52
  294.6 5.3 %fusion.26 = f32[256,3584]{1,0:T(8,128)S(1)} fusion(bf16[1024,3584]{1,0:T(8,128)(2,1)} %bitcast.9, bf16[128,1024]{1,0:T(8,128)(2,1)S(1)} %subtract_convert_fusion, bf16[128,1024]{1,0:T(8,128)(2,1)S(1)} %fusion.30), kind=kOutput, calls=%fused_computation.36 | convolution fusion | flops 1880096768 | bytes 11534336 | tf_op jit(solution)/shard_map/dot_general | solution.py:23
  299.9 0.6 fusion.19
  300.7 1.8 copy-done.1
  302.6 0.6 fusion.20
  303.4 2.6 fusion.54
  306.0 1.3 concatenate.24
  307.3 0.4 copy.43
  307.7 1.3 fusion.42
  309.0 3.1 fusion.9
  312.1 1.3 concatenate.25
  313.4 0.4 copy.44
  314.1 1.3 copy.46
  315.4 10.0 %all-to-all-start.4 = ((f32[128,1,896]{2,1,0:T(1,128)}), f32[128,1,896]{2,1,0:T(1,128)S(1)}, u32[]{:S(2)}, u32[]{:S(2)}) async-start(f32[128,1,896]{2,1,0:T(1,128)} %copy.46), calls=%async_computation.4 | async-start | bytes 917504 | tf_op jit(solution)/shard_map/all_to_all | solution.py:52
  325.4 7.4 %add_multiply_fusion = f32[512,3584]{1,0:T(8,128)} fusion(f32[512,3584]{1,0:T(8,128)} %fusion.5, bf16[128,3584]{1,0:T(8,128)(2,1)S(1)} %copy-done, f32[128,512]{1,0:T(8,128)S(1)} %get-tuple-element.45, f32[128]{0:T(128)S(1)} %get-tuple-element.25, s32[128]{0:T(128)S(1)} %copy-done.13), kind=kOutput, calls=%fused_computation.11 | convolution fusion | flops 473759744 | bytes 15860736 | tf_op jit(solution)/shard_map/dot_general | solution.py:144
  332.8 5.9 %all-to-all-done.4 = f32[128,1,896]{2,1,0:T(1,128)S(1)} async-done(((f32[128,1,896]{2,1,0:T(1,128)}), f32[128,1,896]{2,1,0:T(1,128)S(1)}, u32[]{:S(2)}, u32[]{:S(2)}) %all-to-all-start.4) | async-done | bytes 458784 | tf_op jit(solution)/shard_map/all_to_all | solution.py:52
  339.1 0.7 slice.85
  339.8 0.7 slice.87
  (73 shorter events, 4.2 us)
Async XLA Ops:
  7.2 15.1 %copy-start = (bf16[128,3584]{1,0:T(8,128)(2,1)S(1)}, bf16[128,3584]{1,0:T(8,128)(2,1)}, u32[]{:S(2)}) copy-start(bf16[128,3584]{1,0:T(8,128)(2,1)} %param.10) | copy-start | bytes 2752516
  7.2 173.1 %all-gather.4.cloned.1.call-start = ((), (), s32[]{:S(2)}) async-start(), calls=%async_computation.5 | async-start | bytes 13045760 | tf_op jit(solution)/shard_map/all_gather | solution.py:94
  8.3 10.4 %collective-permute-start = (bf16[28,1792]{1,0:T(8,128)(2,1)S(1)}, bf16[28,1792]{1,0:T(8,128)(2,1)S(1)}, u32[]{:S(2)}, u32[]{:S(2)}) collective-permute-start(bf16[28,1792]{1,0:T(8,128)(2,1)S(1)} %get-tuple-element.32), channel_id=1, source_target_pairs={{0,0},{1,16},{2,1},{3,17},{4,2},{5,18},{6,3},{7,19},{8,4},{9,20},{... | collective-permute-start | bytes 301064 | tf_op jit(solution)/shard_map/ppermute | solution.py:44
  14.5 5.4 %collective-permute-start.1 = (bf16[28,1792]{1,0:T(8,128)(2,1)S(1)}, bf16[28,1792]{1,0:T(8,128)(2,1)S(1)}, u32[]{:S(2)}, u32[]{:S(2)}) collective-permute-start(bf16[28,1792]{1,0:T(8,128)(2,1)S(1)} %get-tuple-element.33), channel_id=1, source_target_pairs={{0,16},{1,0},{2,17},{3,1},{4,18},{5,2},{6,19},{7,3},{8,20},{9,4},{... | collective-permute-start | bytes 301064 | tf_op jit(solution)/shard_map/ppermute | solution.py:45
  20.7 212.4 %all-gather.6.cloned.1.call-start = ((), (), s32[]{:S(2)}) async-start(), calls=%async_computation.6 | async-start | bytes 38535168 | tf_op jit(solution)/shard_map/all_gather | solution.py:115
  24.3 109.4 %copy-start.2 = (bf16[512,3584]{1,0:T(8,128)(2,1)S(1)}, bf16[512,3584]{1,0:T(8,128)(2,1)}, u32[]{:S(2)}) copy-start(bf16[512,3584]{1,0:T(8,128)(2,1)} %param.11) | copy-start | bytes 11010052
  133.8 4.0 %copy-start.6 = (bf16[128,8,3584]{2,1,0:T(8,128)(2,1)}, bf16[128,8,3584]{2,1,0:T(8,128)(2,1)S(1)}, u32[]{:S(2)}) copy-start(bf16[128,8,3584]{2,1,0:T(8,128)(2,1)S(1)} %all_to_all.34) | copy-start | bytes 22020100
  137.8 1.4 copy-start.9
  202.3 5.9 %copy-start.12 = (bf16[3584]{0:T(1024)(128)(2,1)S(1)}, bf16[3584]{0:T(1024)(128)(2,1)}, u32[]{:S(2)}) copy-start(bf16[3584]{0:T(1024)(128)(2,1)} %param.19) | copy-start | bytes 21508
  202.3 92.3 %all-to-all-start.2 = ((bf16[128,8,3584]{2,1,0:T(8,128)(2,1)}), bf16[128,8,3584]{2,1,0:T(8,128)(2,1)}, u32[]{:S(2)}, u32[]{:S(2)}) async-start(bf16[128,8,3584]{2,1,0:T(8,128)(2,1)} %bitcast.61), calls=%async_computation.2 | async-start | bytes 14680064 | tf_op jit(solution)/shard_map/all_to_all | solution.py:52
  208.1 6.4 %copy-start.13 = (s32[128]{0:T(128)S(1)}, s32[128]{0:T(128)}, u32[]{:S(2)}) copy-start(s32[128]{0:T(128)} %param.13) | copy-start | bytes 1540
  208.2 6.4 %copy-start.11 = (bf16[3584,16]{0,1:T(8,128)(2,1)S(1)}, bf16[3584,16]{0,1:T(8,128)(2,1)}, u32[]{:S(2)}) copy-start(bf16[3584,16]{0,1:T(8,128)(2,1)} %param.17) | copy-start | bytes 344068
  214.5 3.3 copy-start.3
  233.1 12.7 %copy-start.4 = (bf16[512,3584]{1,0:T(8,128)(2,1)S(1)}, bf16[512,3584]{1,0:T(8,128)(2,1)}, u32[]{:S(2)}) copy-start(bf16[512,3584]{1,0:T(8,128)(2,1)} %param.14) | copy-start | bytes 11010052
  245.8 10.4 %copy-start.7 = (bf16[512,3584]{0,1:T(8,128)(2,1)S(1)}, bf16[512,3584]{0,1:T(8,128)(2,1)}, u32[]{:S(2)}) copy-start(bf16[512,3584]{0,1:T(8,128)(2,1)} %copy.39) | copy-start | bytes 11010052
  245.8 10.4 %copy-start.10 = (bf16[16,3584]{1,0:T(8,128)(2,1)S(1)}, bf16[16,3584]{1,0:T(8,128)(2,1)}, u32[]{:S(2)}) copy-start(bf16[16,3584]{1,0:T(8,128)(2,1)} %param.18) | copy-start | bytes 344068
  294.6 5.3 %copy-start.5 = (f32[256,3584]{1,0:T(8,128)S(1)}, f32[256,3584]{1,0:T(8,128)}, u32[]{:S(2)}) copy-start(f32[256,3584]{1,0:T(8,128)} %fusion.35) | copy-start | bytes 11010052
  299.9 2.7 copy-start.1
  300.5 2.7 copy-start.8
  315.4 23.3 %all-to-all-start.4 = ((f32[128,1,896]{2,1,0:T(1,128)}), f32[128,1,896]{2,1,0:T(1,128)S(1)}, u32[]{:S(2)}, u32[]{:S(2)}) async-start(f32[128,1,896]{2,1,0:T(1,128)} %copy.46), calls=%async_computation.4 | async-start | bytes 917504 | tf_op jit(solution)/shard_map/all_to_all | solution.py:52
Sparse Core Ops, SparseCore 0:
  20.8 159.4 all-gather.3
  181.9 45.9 all-gather.5
where the time goes:
time: 348 us; the launch traced here: 347 us
  blocking collectives  144 us (41%)
  matrix products  82.2 us (24%)
  waiting for transfers between devices  58.3 us (17%)
  starting transfers between devices  23.3 us (7%)
  local copies, waits for them, and re-layouts  18 us (5%)
  between operations  14.5 us (4%)
  other arithmetic  6.98 us (2%)
    all_to_all x3, blocking collectives, exchange(): return lax.all_to_all(array, PB_PA, split_axis=0, concat_axis=0, tiled=True)  144 us
    dot_general x12, matrix products, dot(): return jnp.dot(a, b, preferred_element_type=f32, **kw)  55.1 us
    all_to_all x2, waiting for transfers between devices, exchange(): return lax.all_to_all(array, PB_PA, split_axis=0, concat_axis=0, tiled=True)  37.9 us
    all_gather x1, waiting for transfers between devices, local(): half_weight = lax.all_gather(weight_rows, CHIPS, axis=0, tiled=True)  16.1 us
    all_to_all x2, starting transfers between devices, exchange(): return lax.all_to_all(array, PB_PA, split_axis=0, concat_axis=0, tiled=True)  15.9 us
    dot_general x1, matrix products, local(): lax.dot_general(far_weight, arrived, product_dims, preferred_element_type...  10.6 us
    unnamed x30, local copies, waits for them, and re-layouts  9.97 us
    dot_general x1, matrix products, local(): lax.dot_general(near_weight, queries, product_dims, preferred_element_typ...  7.38 us
  transfers between devices with their start and end apart: 6, of which 5 were waited for; matrix products, arithmetic and copies ran while one was open for 24% of the time, Pallas kernels for 0%

commit v1 on v0

--- a/solution.py
+++ b/solution.py
@@ -91,7 +91,9 @@
     outgoing = jnp.dot(picks.astype(bf16), queries, preferred_element_type=bf16)
     arrived = exchange(outgoing.reshape(device_count, slot_rows, MODEL_WIDTH))
     arrived = arrived.reshape(-1, MODEL_WIDTH)
-    half_weight = lax.all_gather(weight_rows, CHIPS, axis=0, tiled=True)
+    half_weight = jnp.concatenate(
+        lax.all_to_all(jnp.stack([weight_rows] * lax.axis_size(CHIPS)), CHIPS, 0, 0), axis=0
+    )
     near_scores = dot(queries, passages.T) * score_scale
     near_peak = jnp.max(near_scores, axis=1)
     near_exp = jnp.exp(near_scores - near_peak[:, None])

time: 348 us -> 547 us (1.57)
  waiting for transfers between devices: 58.3 us -> 338 us
  blocking collectives: 144 us -> 18.8 us
  starting transfers between devices: 23.3 us -> 56.2 us
  matrix products: 82.2 us -> 89.3 us
  local copies, waits for them, and re-layouts: 18 us -> 24.2 us
    all_to_all x0 -> x1, waiting for transfers between devices: none -> 210 us  [local(): lax.all_to_all(jnp.stack([weight_rows] * lax.axis_size(CHIPS)), CHIPS, 0, 0)]
    all_to_all x3 -> x1, blocking collectives: 144 us -> 18.8 us  [exchange(): return lax.all_to_all(array, PB_PA, split_axis=0, concat_axis=0, tiled=True)]
    ppermute x1, waiting for transfers between devices: 3.09 us -> 79 us  [gathered_weight_input(): first = lax.ppermute(jnp.where(odd, right, left), PB_PA, same)]
    all_to_all x2 -> x4, starting transfers between devices: 15.9 us -> 44.3 us  [exchange(): return lax.all_to_all(array, PB_PA, split_axis=0, concat_axis=0, tiled=True)]
    all_gather x1 -> x0, waiting for transfers between devices: 16.1 us -> none  [local(): half_weight = lax.all_gather(weight_rows, CHIPS, axis=0, tiled=True)]
    all_to_all x2 -> x4, waiting for transfers between devices: 37.9 us -> 48.8 us  [exchange(): return lax.all_to_all(array, PB_PA, split_axis=0, concat_axis=0, tiled=True)]
    all_to_all x0 -> x1, starting transfers between devices: none -> 5.79 us  [local(): lax.all_to_all(jnp.stack([weight_rows] * lax.axis_size(CHIPS)), CHIPS, 0, 0)]
  transfers between devices with their start and end apart: 6 -> 8, of which waited for: 5 -> 6; matrix products, arithmetic and copies ran while one was open for 24% -> 12% of each run, Pallas kernels for 0% -> 0%
where the time goes in v1:
time: 547 us; the launch traced here: 546 us
  waiting for transfers between devices  338 us (62%)
  matrix products  89.3 us (16%)
  starting transfers between devices  56.2 us (10%)
  local copies, waits for them, and re-layouts  24.2 us (4%)
  blocking collectives  18.8 us (3%)
  between operations  14.5 us (3%)
    all_to_all x1, waiting for transfers between devices, local(): lax.all_to_all(jnp.stack([weight_rows] * lax.axis_size(CHIPS)), CHIPS, 0, 0)  210 us
    ppermute x1, waiting for transfers between devices, gathered_weight_input(): first = lax.ppermute(jnp.where(odd, right, left), PB_PA, same)  79 us
    dot_general x12, matrix products, dot(): return jnp.dot(a, b, preferred_element_type=f32, **kw)  59.3 us
    all_to_all x4, waiting for transfers between devices, exchange(): return lax.all_to_all(array, PB_PA, split_axis=0, concat_axis=0, tiled=True)  48.8 us
    all_to_all x4, starting transfers between devices, exchange(): return lax.all_to_all(array, PB_PA, split_axis=0, concat_axis=0, tiled=True)  44.3 us
    all_to_all x1, blocking collectives, exchange(): return lax.all_to_all(array, PB_PA, split_axis=0, concat_axis=0, tiled=True)  18.8 us
  transfers between devices with their start and end apart: 8, of which 6 were waited for; matrix products, arithmetic and copies ran while one was open for 12% of the time, Pallas kernels for 0%

profile of v1, /device:TPU:1, one launch (start us, length us, event | category | flops | bytes accessed | tf_op | source)
XLA Modules:
  0.0 545.9 jit_solution(11081262769690346727)
XLA Ops:
  7.2 0.8 copy.36
  8.8 5.1 convolution_bitcast_fusion
  13.9 11.9 %all-to-all-start.1 = ((bf16[128,8,3584]{2,1,0:T(8,128)(2,1)}), bf16[128,8,3584]{2,1,0:T(8,128)(2,1)}, u32[]{:S(2)}, u32[]{:S(2)}) async-start(bf16[128,8,3584]{2,1,0:T(8,128)(2,1)} %convolution_bitcast_fusion), calls=%async_computation.1 | async-start | bytes 14680064 | tf_op jit(solution)/shard_map/all_to_all | solution.py:52
  25.9 5.1 collective-permute-start
  30.9 1.0 collective-permute-start.1
  31.9 79.0 %collective-permute-done = bf16[28,1792]{1,0:T(8,128)(2,1)S(1)} collective-permute-done((bf16[28,1792]{1,0:T(8,128)(2,1)S(1)}, bf16[28,1792]{1,0:T(8,128)(2,1)S(1)}, u32[]{:S(2)}, u32[]{:S(2)}) %collective-permute-start) | collective-permute-done | bytes 100384 | tf_op jit(solution)/shard_map/ppermute | solution.py:44
  111.0 1.5 all-to-all-done.1
  112.5 8.1 %multiply_reduce_fusion.1 = (f32[1024]{0:T(1024)S(1)}, f32[1024,512]{0,1:T(8,128)S(1)}) fusion(bf16[512,3584]{1,0:T(8,128)(2,1)} %param.11, bf16[128,8,3584]{2,1,0:T(8,128)(2,1)} %all-to-all-done.1), kind=kOutput, calls=%fused_computation.27 | convolution fusion | flops 3759143936 | bytes 13111296 | tf_op jit(solution)/shard_map/dot_general | solution.py:23
  120.7 0.4 fusion.17
  121.1 1.0 copy-done.8
  122.0 6.1 %divide_convert_fusion = bf16[1024,3584]{1,0:T(8,128)(2,1)} fusion(f32[1024]{0:T(1024)S(1)} %fusion.17, bf16[512,3584]{1,0:T(8,128)(2,1)S(1)} %copy-done.2, f32[1024,512]{0,1:T(8,128)S(1)} %get-tuple-element.47, f32[1024]{0:T(1024)S(1)} %get-tuple-element.46), kind=kOutput, calls=%fused_computation | convolution fusion | flops 3767009280 | bytes 13115392 | tf_op jit(solution)/shard_map/dot_general | solution.py:23
  128.1 0.7 all_to_all.27
  128.9 16.6 %all-to-all-start.2 = ((f32[128,1,8]{2,1,0:T(1,128)}), f32[128,1,8]{2,1,0:T(1,128)S(1)}, u32[]{:S(2)}, u32[]{:S(2)}) async-start(f32[128,1,8]{2,1,0:T(1,128)} %bitcast.8), calls=%async_computation.2 | async-start | bytes 131072 | tf_op jit(solution)/shard_map/all_to_all | solution.py:52
  145.6 9.5 %all-to-all-done.2 = f32[128,1,8]{2,1,0:T(1,128)S(1)} async-done(((f32[128,1,8]{2,1,0:T(1,128)}), f32[128,1,8]{2,1,0:T(1,128)S(1)}, u32[]{:S(2)}, u32[]{:S(2)}) %all-to-all-start.2) | async-done | bytes 4128 | tf_op jit(solution)/shard_map/all_to_all | solution.py:52
  155.0 5.4 stack.2
  160.4 5.8 %all-to-all-start = ((bf16[64,56,1792]{2,1,0:T(8,128)(2,1)}), bf16[64,56,1792]{2,1,0:T(8,128)(2,1)}, u32[]{:S(2)}, u32[]{:S(2)}) async-start(bf16[64,56,1792]{2,1,0:T(8,128)(2,1)} %stack.2), calls=%async_computation | async-start | bytes 25690112 | tf_op jit(solution)/shard_map/all_to_all | solution.py:95
  166.3 0.5 broadcast.138
  166.8 0.8 reduce.7
  167.7 209.8 %all-to-all-done = bf16[64,56,1792]{2,1,0:T(8,128)(2,1)} async-done(((bf16[64,56,1792]{2,1,0:T(8,128)(2,1)}), bf16[64,56,1792]{2,1,0:T(8,128)(2,1)}, u32[]{:S(2)}, u32[]{:S(2)}) %all-to-all-start) | async-done | bytes 12845088 | tf_op jit(solution)/shard_map/all_to_all | solution.py:95
  377.8 3.4 fusion.72
  381.4 0.4 select_reduce_fusion.2
  382.2 18.8 %all_to_all.39 = f32[128,1,8]{2,1,0:T(1,128)S(1)} all-to-all(f32[128,1,8]{2,1,0:T(1,128)S(1)} %bitcast.63), channel_id=1, replica_groups=mesh['pb_0'=4,'pb_1'=2,'pa_0'=4,'pa_1'=4] {'pb_0','pb_1','pa_0','pa_1'}, dimensions={0} | all-to-all | bytes 8192 | tf_op jit(solution)/shard_map/all_to_all | solution.py:52
  401.0 5.7 %all-to-all-start.3 = ((bf16[128,8,3584]{2,1,0:T(8,128)(2,1)}), bf16[128,8,3584]{2,1,0:T(8,128)(2,1)}, u32[]{:S(2)}, u32[]{:S(2)}) async-start(bf16[128,8,3584]{2,1,0:T(8,128)(2,1)} %bitcast.62), calls=%async_computation.3 | async-start | bytes 14680064 | tf_op jit(solution)/shard_map/all_to_all | solution.py:52
  406.8 6.4 %copy.39 = bf16[512,3584]{0,1:T(8,128)(2,1)} copy(bf16[512,3584]{1,0:T(8,128)(2,1)} %param.15) | data formatting | bytes 7340032 | tf_op args[5]
  413.3 3.2 convolution_convert_fusion
  416.5 3.1 fusion.35
  420.3 0.8 reduce.8
  421.2 10.6 %fusion.5 = f32[512,3584]{1,0:T(8,128)} fusion(bf16[128,8,3584]{2,1,0:T(8,128)(2,1)} %all-to-all-done.1, f32[1024,512]{0,1:T(8,128)} %copy-done.8, f32[1024]{0:T(1024)S(1)} %sub.236), kind=kOutput, calls=%fused_computation.7 | convolution fusion | flops 3759669248 | bytes 16781312 | tf_op jit(solution)/shard_map/dot_general | solution.py:145
  431.8 12.7 %fusion.10 = f32[512,1792]{0,1:T(8,128)S(1)} fusion(bf16[512,3584]{1,0:T(8,128)(2,1)} %param.14, bf16[7168,1792]{1,0:T(8,128)(2,1)} %all-gather.3.cloned.1.call-done), kind=kOutput, calls=%fused_computation.16 | convolution fusion | flops 6576668672 | bytes 20185088 | tf_op jit(solution)/shard_map/dot_general | solution.py:23
  444.5 10.3 %fusion.13 = f32[512,1792]{0,1:T(8,128)S(1)} fusion(bf16[512,3584]{1,0:T(8,128)(2,1)S(1)} %copy-done.4, bf16[7168,1792]{1,0:T(8,128)(2,1)} %all-gather.3.cloned.1.call-done), kind=kOutput, calls=%fused_computation.17 | convolution fusion | flops 6576668672 | bytes 20185088 | tf_op jit(solution)/shard_map/dot_general | solution.py:23
  454.9 3.5 multiply_reduce_fusion
  458.7 2.6 fusion.73
  461.3 31.9 %all-to-all-done.3 = bf16[128,8,3584]{2,1,0:T(8,128)(2,1)} async-done(((bf16[128,8,3584]{2,1,0:T(8,128)(2,1)}), bf16[128,8,3584]{2,1,0:T(8,128)(2,1)}, u32[]{:S(2)}, u32[]{:S(2)}) %all-to-all-start.3) | async-done | bytes 7340064 | tf_op jit(solution)/shard_map/all_to_all | solution.py:52
  493.2 5.3 fusion.26
  498.5 0.6 fusion.19
  499.3 1.8 copy-done.1
  501.2 0.6 fusion.20
  502.0 2.6 fusion.54
  504.6 1.3 concatenate.24
  506.3 1.3 fusion.42
  507.6 3.1 fusion.9
  510.7 1.3 concatenate.25
  512.7 1.3 copy.46
  514.0 10.0 %all-to-all-start.5 = ((f32[128,1,896]{2,1,0:T(1,128)}), f32[128,1,896]{2,1,0:T(1,128)S(1)}, u32[]{:S(2)}, u32[]{:S(2)}) async-start(f32[128,1,896]{2,1,0:T(1,128)} %copy.46), calls=%async_computation.5 | async-start | bytes 917504 | tf_op jit(solution)/shard_map/all_to_all | solution.py:52
  524.0 7.4 %add_multiply_fusion = f32[512,3584]{1,0:T(8,128)} fusion(f32[512,3584]{1,0:T(8,128)} %fusion.5, bf16[128,3584]{1,0:T(8,128)(2,1)S(1)} %copy-done, f32[128,512]{1,0:T(8,128)S(1)} %get-tuple-element.45, f32[128]{0:T(128)S(1)} %get-tuple-element.25, s32[128]{0:T(128)S(1)} %copy-done.13), kind=kOutput, calls=%fused_computation.11 | convolution fusion | flops 473759744 | bytes 15860736 | tf_op jit(solution)/shard_map/dot_general | solution.py:146
  531.4 5.9 %all-to-all-done.5 = f32[128,1,896]{2,1,0:T(1,128)S(1)} async-done(((f32[128,1,896]{2,1,0:T(1,128)}), f32[128,1,896]{2,1,0:T(1,128)S(1)}, u32[]{:S(2)}, u32[]{:S(2)}) %all-to-all-start.5) | async-done | bytes 458784 | tf_op jit(solution)/shard_map/all_to_all | solution.py:52
  537.7 0.7 slice.85
  538.4 0.7 slice.87
  (75 shorter events, 4.9 us)
Async XLA Ops:
  7.2 1.6 copy-start
  13.9 11.9 %copy-start.10 = (bf16[28,3584]{1,0:T(8,128)(2,1)S(1)}, bf16[28,3584]{1,0:T(8,128)(2,1)}, u32[]{:S(2)}) copy-start(bf16[28,3584]{1,0:T(8,128)(2,1)} %param.16) | copy-start | bytes 602116
  13.9 98.6 %all-to-all-start.1 = ((bf16[128,8,3584]{2,1,0:T(8,128)(2,1)}), bf16[128,8,3584]{2,1,0:T(8,128)(2,1)}, u32[]{:S(2)}, u32[]{:S(2)}) async-start(bf16[128,8,3584]{2,1,0:T(8,128)(2,1)} %convolution_bitcast_fusion), calls=%async_computation.1 | async-start | bytes 14680064 | tf_op jit(solution)/shard_map/all_to_all | solution.py:52
  25.9 85.1 %collective-permute-start = (bf16[28,1792]{1,0:T(8,128)(2,1)S(1)}, bf16[28,1792]{1,0:T(8,128)(2,1)S(1)}, u32[]{:S(2)}, u32[]{:S(2)}) collective-permute-start(bf16[28,1792]{1,0:T(8,128)(2,1)S(1)} %get-tuple-element.32), channel_id=1, source_target_pairs={{0,0},{1,16},{2,1},{3,17},{4,2},{5,18},{6,3},{7,19},{8,4},{9,20},{... | collective-permute-start | bytes 301064 | tf_op jit(solution)/shard_map/ppermute | solution.py:44
  30.9 80.1 %collective-permute-start.1 = (bf16[28,1792]{1,0:T(8,128)(2,1)S(1)}, bf16[28,1792]{1,0:T(8,128)(2,1)S(1)}, u32[]{:S(2)}, u32[]{:S(2)}) collective-permute-start(bf16[28,1792]{1,0:T(8,128)(2,1)S(1)} %get-tuple-element.33), channel_id=1, source_target_pairs={{0,16},{1,0},{2,17},{3,1},{4,18},{5,2},{6,19},{7,3},{8,20},{9,4},{... | collective-permute-start | bytes 301064 | tf_op jit(solution)/shard_map/ppermute | solution.py:45
  112.5 9.5 %copy-start.2 = (bf16[512,3584]{1,0:T(8,128)(2,1)S(1)}, bf16[512,3584]{1,0:T(8,128)(2,1)}, u32[]{:S(2)}) copy-start(bf16[512,3584]{1,0:T(8,128)(2,1)} %param.11) | copy-start | bytes 11010052
  120.7 1.4 copy-start.8
  128.9 26.2 %all-to-all-start.2 = ((f32[128,1,8]{2,1,0:T(1,128)}), f32[128,1,8]{2,1,0:T(1,128)S(1)}, u32[]{:S(2)}, u32[]{:S(2)}) async-start(f32[128,1,8]{2,1,0:T(1,128)} %bitcast.8), calls=%async_computation.2 | async-start | bytes 131072 | tf_op jit(solution)/shard_map/all_to_all | solution.py:52
  160.4 217.1 %all-to-all-start = ((bf16[64,56,1792]{2,1,0:T(8,128)(2,1)}), bf16[64,56,1792]{2,1,0:T(8,128)(2,1)}, u32[]{:S(2)}, u32[]{:S(2)}) async-start(bf16[64,56,1792]{2,1,0:T(8,128)(2,1)} %stack.2), calls=%async_computation | async-start | bytes 25690112 | tf_op jit(solution)/shard_map/all_to_all | solution.py:95
  166.2 265.5 %all-gather.3.cloned.1.call-start = ((), (), s32[]{:S(2)}) async-start(), calls=%async_computation.6 | async-start | bytes 38535168 | tf_op jit(solution)/shard_map/all_gather | solution.py:117
  401.0 5.7 %copy-start.12 = (bf16[3584]{0:T(1024)(128)(2,1)S(1)}, bf16[3584]{0:T(1024)(128)(2,1)}, u32[]{:S(2)}) copy-start(bf16[3584]{0:T(1024)(128)(2,1)} %param.19) | copy-start | bytes 21508
  401.0 92.2 %all-to-all-start.3 = ((bf16[128,8,3584]{2,1,0:T(8,128)(2,1)}), bf16[128,8,3584]{2,1,0:T(8,128)(2,1)}, u32[]{:S(2)}, u32[]{:S(2)}) async-start(bf16[128,8,3584]{2,1,0:T(8,128)(2,1)} %bitcast.62), calls=%async_computation.3 | async-start | bytes 14680064 | tf_op jit(solution)/shard_map/all_to_all | solution.py:52
  406.7 6.5 %copy-start.13 = (s32[128]{0:T(128)S(1)}, s32[128]{0:T(128)}, u32[]{:S(2)}) copy-start(s32[128]{0:T(128)} %param.13) | copy-start | bytes 1540
  406.8 6.5 %copy-start.11 = (bf16[3584,16]{0,1:T(8,128)(2,1)S(1)}, bf16[3584,16]{0,1:T(8,128)(2,1)}, u32[]{:S(2)}) copy-start(bf16[3584,16]{0,1:T(8,128)(2,1)} %param.17) | copy-start | bytes 344068
  413.2 3.3 copy-start.3
  431.8 12.7 %copy-start.4 = (bf16[512,3584]{1,0:T(8,128)(2,1)S(1)}, bf16[512,3584]{1,0:T(8,128)(2,1)}, u32[]{:S(2)}) copy-start(bf16[512,3584]{1,0:T(8,128)(2,1)} %param.14) | copy-start | bytes 11010052
  444.5 10.4 %copy-start.6 = (bf16[512,3584]{0,1:T(8,128)(2,1)S(1)}, bf16[512,3584]{0,1:T(8,128)(2,1)}, u32[]{:S(2)}) copy-start(bf16[512,3584]{0,1:T(8,128)(2,1)} %copy.39) | copy-start | bytes 11010052
  444.5 10.4 %copy-start.9 = (bf16[16,3584]{1,0:T(8,128)(2,1)S(1)}, bf16[16,3584]{1,0:T(8,128)(2,1)}, u32[]{:S(2)}) copy-start(bf16[16,3584]{1,0:T(8,128)(2,1)} %param.18) | copy-start | bytes 344068
  493.2 5.3 copy-start.5
  498.5 2.7 copy-start.1
  499.1 2.7 copy-start.7
  514.0 23.3 %all-to-all-start.5 = ((f32[128,1,896]{2,1,0:T(1,128)}), f32[128,1,896]{2,1,0:T(1,128)S(1)}, u32[]{:S(2)}, u32[]{:S(2)}) async-start(f32[128,1,896]{2,1,0:T(1,128)} %copy.46), calls=%async_computation.5 | async-start | bytes 917504 | tf_op jit(solution)/shard_map/all_to_all | solution.py:52
Sparse Core Ops, SparseCore 0:
  377.7 47.4 all-gather.2
